TPU v7x, 32 devices: a whole 2x2x4 slice. The times are simulated.
32 devices in a mesh: groups: 2 (over x), seq: 16 (over z, y, core).
Axes of the slice: x: 2, y: 2, z: 4, core: 2. Of those that a mesh axis runs over, the one named last changes fastest.
Arguments:
- tokens: bfloat16 [1024, 512, 512], P(('groups', 'seq')), parts along dimension 0, may hold values from -6 to 6
- cotangent: bfloat16 [1024, 512, 512], P('groups', 'seq'), parts along dimension 0, may hold values from -6 to 6
- w_first: bfloat16 [512, 512], P('seq'), may hold values from -0.25 to 0.25
- w_second: bfloat16 [512, 512], P('seq'), may hold values from -0.25 to 0.25
- mask_first: int32 [4, 4], replicated, may hold values from 0 to 1, as said below
- mask_second: int32 [4, 4], replicated, may hold values from 0 to 1, as said below
- gate_values: bfloat16 [1024, 512], P(('groups', 'seq')), parts along dimension 0, may hold values from -4 to 4
Outputs:
- grad_tokens: bfloat16 [1024, 512, 512], P(('groups', 'seq')), parts along dimension 0
- grad_first: float32 [1024, 512], P(('groups', 'seq')), parts along dimension 0
- grad_second: float32 [1024, 512], P(('groups', 'seq')), parts along dimension 0
There are 2 independent parts, one for each index of `groups`. A program takes and returns all parts, laid end to end along the dimension named above; an argument that names none is the same for every part. Nothing has to cross between parts.
Inputs may be any that keep to these rules, and one draw needn't show every extreme that they name: `mask_first`: the diagonal blocks of each factor are always kept. `mask_second`: the diagonal blocks of each factor are always kept.
All inputs are finite; a program needn't handle non-finite values.
Results may differ from a plain program's by a relative error of at most 0.0054.
Values may be sent and summed in bfloat16 or wider, within the bound.
A program may use at most 320 MiB of HBM per device.

v0:
```python
import math
import jax
import jax.numpy as jnp
from jax import lax
from jax.sharding import PartitionSpec as P

BLK = 128


def expand_rows(mask, row_ids, extent):
    labels = jnp.arange(mask.shape[0], dtype=jnp.int32)
    row_pick = ((row_ids // BLK)[:, None] == labels[None, :]).astype(jnp.float32)
    col_pick = ((jnp.arange(extent, dtype=jnp.int32) // BLK)[:, None] == labels[None, :]).astype(
        jnp.float32
    )
    return jnp.dot(jnp.dot(row_pick, mask.astype(jnp.float32)), col_pick.T)


def per_device(tokens, cotangent, w_first, w_second, mask_first, mask_second, gate_values):
    position = lax.axis_index("seq")
    extent = tokens.shape[1]
    channels = tokens.shape[2]
    shard_rows = w_first.shape[0]
    row_ids = position * shard_rows + jnp.arange(shard_rows, dtype=jnp.int32)
    keep_first = expand_rows(mask_first, row_ids, extent)
    keep_second = expand_rows(mask_second, row_ids, extent)
    local_first = (w_first.astype(jnp.float32) * keep_first).astype(jnp.bfloat16)
    local_second = (w_second.astype(jnp.float32) * keep_second).astype(jnp.bfloat16)
    full = lax.all_gather(jnp.stack([local_first, local_second]), "seq", axis=1, tiled=True)
    full_first, full_second = (full[0], full[1])
    shards = extent // shard_rows
    flat_cot = cotangent.reshape(extent, -1)
    back_flat = lax.dot_general(
        full_second, flat_cot, (((0,), (0,)), ((), ())), preferred_element_type=jnp.float32
    )
    back_col = back_flat.astype(jnp.bfloat16).reshape(cotangent.shape)
    back_rows = lax.all_to_all(back_col, "seq", split_axis=0, concat_axis=1, tiled=True)
    tokens_late, back_col = lax.optimization_barrier((tokens, back_col))
    gate_full = gate_values.astype(jnp.float32)[:, :, None]
    gated = tokens_late.astype(jnp.float32) * gate_full
    hidden = jnp.einsum("ijc,kj->ikc", tokens_late, full_first, preferred_element_type=jnp.float32)
    mixed = (hidden * gated).astype(jnp.bfloat16)
    mixed, back_rows = lax.optimization_barrier((mixed, back_rows))
    columns = lax.all_to_all(mixed, "seq", split_axis=1, concat_axis=0, tiled=True)
    flat_cols = columns.reshape(extent, -1)
    back_float = back_rows.astype(jnp.float32)
    back_hidden = (back_float * gated).astype(jnp.bfloat16)
    direct = gate_full * back_float * hidden
    through = jnp.einsum("ikc,kj->ijc", back_hidden, full_first, preferred_element_type=jnp.float32)
    grad_tokens = (direct + through).astype(jnp.bfloat16)
    summed_first = lax.psum_scatter(
        jnp.einsum("ikc,ijc->kj", back_hidden, tokens_late, preferred_element_type=jnp.float32),
        "seq",
        scatter_dimension=0,
        tiled=True,
    )
    part_second = lax.dot_general(
        flat_cot, flat_cols, (((1,), (1,)), ((), ())), preferred_element_type=jnp.float32
    )
    spread = lax.all_to_all(
        part_second.reshape(shards, shard_rows, extent),
        "seq",
        split_axis=0,
        concat_axis=0,
        tiled=True,
    )
    summed_second = jnp.sum(spread, axis=0)
    factor = 1.0 / math.sqrt(extent * channels)
    grad_first = keep_first * summed_first * factor
    grad_second = keep_second * summed_second * factor
    return (grad_tokens, grad_first, grad_second)


def solution(mesh):
    in_specs = (
        P(("groups", "seq"), None, None),
        P("groups", "seq", None),
        P("seq", None),
        P("seq", None),
        P(),
        P(),
        P(("groups", "seq"), None),
    )
    out_specs = (
        P(("groups", "seq"), None, None),
        P(("groups", "seq"), None),
        P(("groups", "seq"), None),
    )
    return jax.shard_map(
        per_device, mesh=mesh, in_specs=in_specs, out_specs=out_specs, check_vma=False
    )
```

profile of v0, /device:TPU:0, one launch (start us, length us, event | category | flops | bytes accessed | tf_op | source)
XLA Modules:
  0.0 964.3 jit_solution(4726643977585891241)
XLA Ops:
  7.2 1.1 fusion.14
  8.3 1.1 fusion.17
  9.4 0.8 fusion.23
  10.2 0.6 pad_maximum_fusion
  10.9 18.5 %copy.21 = bf16[64,8,32,512]{3,1,2,0:T(8,128)(2,1)} copy(bf16[64,8,32,512]{3,2,1,0:T(8,128)(2,1)} %bitcast.58) | data formatting | bytes 33554432
  29.3 22.4 %all-gather.2.cloned.1.call-done = bf16[2,512,512]{2,1,0:T(8,128)(2,1)} async-done(((bf16[2,32,512]{2,1,0:T(8,128)(2,1)}), bf16[2,512,512]{2,1,0:T(8,128)(2,1)}) %all-gather.2.cloned.1.call-update) | async-done | bytes 1048592 | tf_op jit(solution)/shard_map/all_gather | solution.py:29
  51.7 15.8 %convolution_convert_fusion = bf16[512,16384]{1,0:T(8,128)(2,1)} fusion(bf16[512,16384]{1,0:T(8,128)(2,1)} %bitcast.53, bf16[2,512,512]{2,1,0:T(8,128)(2,1)} %all-gather.2.cloned.1.call-done), kind=kOutput, calls=%fused_computation.9 | convolution fusion | flops 8598323200 | bytes 34078720 | tf_op jit(solution)/shard_map/dot_general | solution.py:33
  67.5 16.6 %copy.22 = bf16[64,8,32,512]{3,2,1,0:T(8,128)(2,1)} copy(bf16[64,8,32,512]{3,1,2,0:T(8,128)(2,1)} %bitcast.55) | data formatting | bytes 33554432
  84.0 5.5 all-to-all-start
  89.6 28.2 %fusion.4 = (bf16[32,512,512]{2,1,0:T(8,128)(2,1)}, f32[512,32,512]{2,0,1:T(8,128)}) fusion(bf16[32,512,512]{2,1,0:T(8,128)(2,1)} %param.7, f32[32,512]{1,0:T(8,128)S(1)} %convert_element_type.43, bf16[2,512,512]{2,1,0:T(8,128)(2,1)S(1)} %copy-done.1), kind=kOutput, calls=%fused_computation.7 | convolution fusion | flops 8623489024 | bytes 84475904 | tf_op jit(solution)/shard_map/ijc,kj->ikc/dot_general | solution.py:41
  117.7 268.3 %all-to-all-done = bf16[512,32,512]{2,1,0:T(8,128)(2,1)} async-done(((bf16[512,32,512]{2,1,0:T(8,128)(2,1)}), bf16[512,32,512]{2,1,0:T(8,128)(2,1)}, u32[]{:S(2)}, u32[]{:S(2)}) %all-to-all-start) | async-done | bytes 16777248 | tf_op jit(solution)/shard_map/all_to_all | solution.py:37
  386.0 15.1 %copy.15 = bf16[16,32,32,512]{3,2,0,1:T(8,128)(2,1)} copy(bf16[16,32,32,512]{3,2,1,0:T(8,128)(2,1)} %bitcast.6) | data formatting | bytes 33554432 | tf_op jit(solution)/shard_map/all_to_all | solution.py:37
  401.1 1.8 copy-done
  402.9 26.5 %copy.17 = bf16[32,512,512]{2,0,1:T(8,128)(2,1)} copy(bf16[32,512,512]{2,1,0:T(8,128)(2,1)S(1)} %copy-done) | data formatting | bytes 33554432 | tf_op jit(solution)/shard_map/optimization_barrier | solution.py:43
  429.4 70.2 %all-to-all-start.1 = ((bf16[32,512,512]{2,0,1:T(8,128)(2,1)}), bf16[32,512,512]{2,0,1:T(8,128)(2,1)}, u32[]{:S(2)}, u32[]{:S(2)}) async-start(bf16[32,512,512]{2,0,1:T(8,128)(2,1)} %copy.17), calls=%async_computation.2 | async-start | bytes 33554432 | tf_op jit(solution)/shard_map/all_to_all | solution.py:44
  499.9 24.1 %fusion.11 = f32[512,512]{1,0:T(8,128)} fusion(bf16[32,512,512]{2,1,0:T(8,128)(2,1)} %param.7, bf16[32,512,512]{2,1,0:T(8,128)(2,1)} %bitcast.59, f32[32,512]{1,0:T(8,128)S(1)} %convert_element_type.43), kind=kOutput, calls=%fused_computation.12 | convolution fusion | flops 8631877632 | bytes 34668544 | tf_op jit(solution)/shard_map/ikc,ijc->kj/dot_general | solution.py:52
  524.1 278.7 %all-to-all-done.1 = bf16[32,512,512]{2,0,1:T(8,128)(2,1)} async-done(((bf16[32,512,512]{2,0,1:T(8,128)(2,1)}), bf16[32,512,512]{2,0,1:T(8,128)(2,1)}, u32[]{:S(2)}, u32[]{:S(2)}) %all-to-all-start.1) | async-done | bytes 16777248 | tf_op jit(solution)/shard_map/all_to_all | solution.py:44
  802.8 15.8 %copy.18 = bf16[32,16,32,512]{3,2,0,1:T(8,128)(2,1)S(1)} copy(bf16[32,16,32,512]{3,0,2,1:T(8,128)(2,1)} %bitcast.12) | data formatting | bytes 33554432 | tf_op jit(solution)/shard_map/all_to_all | solution.py:44
  818.6 12.2 %copy.23 = bf16[64,8,32,512]{3,1,2,0:T(8,128)(2,1)} copy(bf16[64,8,32,512]{3,2,1,0:T(8,128)(2,1)S(1)} %bitcast.57) | data formatting | bytes 33554432
  830.8 18.0 %fusion.36 = f32[512,512]{0,1:T(8,128)} fusion(bf16[512,16384]{1,0:T(8,128)(2,1)} %bitcast.61, bf16[512,16384]{1,0:T(8,128)(2,1)} %bitcast.54), kind=kOutput, calls=%fused_computation.46 | convolution fusion | flops 8589934592 | bytes 34603008 | tf_op jit(solution)/shard_map/dot_general | solution.py:57
  848.9 70.2 %all-to-all-start.2 = ((f32[16,32,512]{2,1,0:T(8,128)}), f32[16,32,512]{2,1,0:T(8,128)S(1)}, u32[]{:S(2)}, u32[]{:S(2)}) async-start(f32[16,32,512]{2,1,0:T(8,128)} %bitcast.15), calls=%async_computation.3 | async-start | bytes 2097152 | tf_op jit(solution)/shard_map/all_to_all | solution.py:60
  919.1 36.2 %fusion.2 = bf16[32,512,512]{2,1,0:T(8,128)(2,1)} fusion(bf16[32,512,512]{2,1,0:T(8,128)(2,1)} %bitcast.60, f32[512,32,512]{2,0,1:T(8,128)} %get-tuple-element.10, f32[32,512]{1,0:T(8,128)S(1)} %convert_element_type.43, bf16[32,512,512]{2,1,0:T(8,128)(2,1)} %param.7, bf16[2,512,512]{2,1,0:T(8,128)(2,1)S(1)} %copy-done.1), kind=kOutput, calls=%fused_computation.4 | convolution fusion | flops 8673820672 | bytes 101318656 | tf_op jit(solution)/shard_map/ikc,kj->ijc/dot_general | solution.py:49
  955.3 1.5 multiply_multiply_fusion.1
  956.9 0.6 multiply_multiply_fusion
  (23 shorter events, 0.5 us)
Async XLA Ops:
  7.2 44.5 %all-gather.2.cloned.1.call-start = ((), (), s32[]{:S(2)}) async-start(), calls=%async_computation.4 | async-start | bytes 1114112 | tf_op jit(solution)/shard_map/all_gather | solution.py:29
  8.3 21.0 %copy-start.2 = (f32[32,512]{1,0:T(8,128)}, f32[32,512]{1,0:T(8,128)S(1)}, u32[]{:S(2)}) copy-start(f32[32,512]{1,0:T(8,128)S(1)} %fusion.14) | copy-start | bytes 196612
  9.4 19.9 %copy-start.4 = (f32[32,512]{1,0:T(8,128)}, f32[32,512]{1,0:T(8,128)S(1)}, u32[]{:S(2)}) copy-start(f32[32,512]{1,0:T(8,128)S(1)} %fusion.17) | copy-start | bytes 196612
  84.0 5.5 copy-start.6
  84.0 5.5 copy-start.1
  84.0 302.0 %all-to-all-start = ((bf16[512,32,512]{2,1,0:T(8,128)(2,1)}), bf16[512,32,512]{2,1,0:T(8,128)(2,1)}, u32[]{:S(2)}, u32[]{:S(2)}) async-start(bf16[512,32,512]{2,1,0:T(8,128)(2,1)} %bitcast.56), calls=%async_computation | async-start | bytes 33554432 | tf_op jit(solution)/shard_map/all_to_all | solution.py:37
  386.0 16.9 %copy-start = (bf16[32,512,512]{2,1,0:T(8,128)(2,1)S(1)}, bf16[32,512,512]{2,1,0:T(8,128)(2,1)}, u32[]{:S(2)}) copy-start(bf16[32,512,512]{2,1,0:T(8,128)(2,1)} %get-tuple-element.8) | copy-start | bytes 50331652
  429.4 373.4 %all-to-all-start.1 = ((bf16[32,512,512]{2,0,1:T(8,128)(2,1)}), bf16[32,512,512]{2,0,1:T(8,128)(2,1)}, u32[]{:S(2)}, u32[]{:S(2)}) async-start(bf16[32,512,512]{2,0,1:T(8,128)(2,1)} %copy.17), calls=%async_computation.2 | async-start | bytes 33554432 | tf_op jit(solution)/shard_map/all_to_all | solution.py:44
  499.7 455.6 %reduce-scatter.2.cloned.1.call-start = ((), (), s32[]{:S(2)}) async-start(), calls=%async_computation.5 | async-start | bytes 1114112 | tf_op jit(solution)/shard_map/reduce_scatter | solution.py:51
  848.9 107.9 %all-to-all-start.2 = ((f32[16,32,512]{2,1,0:T(8,128)}), f32[16,32,512]{2,1,0:T(8,128)S(1)}, u32[]{:S(2)}, u32[]{:S(2)}) async-start(f32[16,32,512]{2,1,0:T(8,128)} %bitcast.15), calls=%async_computation.3 | async-start | bytes 2097152 | tf_op jit(solution)/shard_map/all_to_all | solution.py:60
  919.1 36.2 %copy-start.5 = (f32[32,512]{1,0:T(8,128)S(1)}, f32[32,512]{1,0:T(8,128)}, u32[]{:S(2)}) copy-start(f32[32,512]{1,0:T(8,128)} %copy-done.4) | copy-start | bytes 196612
  919.1 37.7 %copy-start.3 = (f32[32,512]{1,0:T(8,128)S(1)}, f32[32,512]{1,0:T(8,128)}, u32[]{:S(2)}) copy-start(f32[32,512]{1,0:T(8,128)} %copy-done.2) | copy-start | bytes 196612
Sparse Core Ops, SparseCore 0:
  11.0 40.6 all-gather.1
  524.2 257.9 reduce-scatter.1
where the time goes:
time: 965 us; the launch traced here: 964 us
  waiting for transfers between devices  569 us (59%)
  starting transfers between devices  146 us (15%)
  matrix products  124 us (13%)
  local copies, waits for them, and re-layouts  106 us (11%)
  between operations  14.2 us (1%)
    all_to_all x1, waiting for transfers between devices, per_device(): lax.all_to_all(mixed, 'seq', split_axis=1, concat_axis=0, tiled=True)  279 us
    all_to_all x1, waiting for transfers between devices, per_device(): lax.all_to_all(back_col, 'seq', split_axis=0, concat_axis=1, tiled=True)  268 us
    all_to_all x1, starting transfers between devices, per_device(): lax.all_to_all(part_second.reshape(shards, shard_rows, extent), 'seq', sp...  70.2 us
    all_to_all x1, starting transfers between devices, per_device(): lax.all_to_all(mixed, 'seq', split_axis=1, concat_axis=0, tiled=True)  70.2 us
    unnamed x17, local copies, waits for them, and re-layouts  49 us
    dot_general x1, matrix products, per_device(): jnp.einsum('ikc,kj->ijc', back_hidden, full_first, preferred_element_type...  36.2 us
    dot_general x1, matrix products, per_device(): jnp.einsum('ijc,kj->ikc', tokens_late, full_first, preferred_element_type...  28.2 us
    optimization_barrier x1, local copies, waits for them, and re-layouts, per_device(): mixed, back_rows = lax.optimization_barrier((mixed, back_rows))  26.5 us
  transfers between devices with their start and end apart: 5, of which 3 were waited for; matrix products, arithmetic and copies ran while one was open for 16% of the time, Pallas kernels for 0%

commit v1 on v0

--- a/solution.py
+++ b/solution.py
@@ -5,6 +5,20 @@
 from jax.sharding import PartitionSpec as P
 
 BLK = 128
+
+
+def kinds_turn(packet, axis_tag, in_dim):
+    part_now, z = (lax.axis_size(axis_tag), lax.axis_index(axis_tag))
+    extra, h_now = (packet, 1)
+    while h_now < part_now:
+        upper = lax.ppermute(
+            extra, axis_name=axis_tag, perm=[(m, m ^ h_now) for m in range(part_now)]
+        )
+        local_next = jnp.concatenate([extra, upper], axis=in_dim)
+        s_next = jnp.concatenate([upper, extra], axis=in_dim)
+        extra = jnp.where(z & h_now == 0, local_next, s_next)
+        h_now = 2 * h_now
+    return extra
 
 
 def expand_rows(mask, row_ids, extent):
@@ -26,7 +40,7 @@
     keep_second = expand_rows(mask_second, row_ids, extent)
     local_first = (w_first.astype(jnp.float32) * keep_first).astype(jnp.bfloat16)
     local_second = (w_second.astype(jnp.float32) * keep_second).astype(jnp.bfloat16)
-    full = lax.all_gather(jnp.stack([local_first, local_second]), "seq", axis=1, tiled=True)
+    full = kinds_turn(jnp.stack([local_first, local_second]), "seq", 1)
     full_first, full_second = (full[0], full[1])
     shards = extent // shard_rows
     flat_cot = cotangent.reshape(extent, -1)

time: 965 us -> 968 us (level)
    all_gather x1 -> x0, waiting for transfers between devices: 22.4 us -> none  [per_device(): lax.all_gather(jnp.stack([local_first, local_second]), 'seq', axis=1, til...]
    ppermute x0 -> x4, waiting for transfers between devices: none -> 14.6 us  [kinds_turn(): lax.ppermute(extra, axis_name=axis_tag, perm=[(m, m ^ h_now) for m in ran...]
    unnamed x17 -> x15, local copies, waits for them, and re-layouts: 49 us -> 49 us
  transfers between devices with their start and end apart: 5 -> 8, of which waited for: 3 -> 6; matrix products, arithmetic and copies ran while one was open for 16% -> 16% of each run, Pallas kernels for 0% -> 0%
where the time goes in v1:
time: 968 us; the launch traced here: 967 us
  waiting for transfers between devices  562 us (58%)
  starting transfers between devices  154 us (16%)
  matrix products  127 us (13%)
  local copies, waits for them, and re-layouts  106 us (11%)
  between operations  14.2 us (1%)
    all_to_all x1, waiting for transfers between devices, per_device(): lax.all_to_all(mixed, 'seq', split_axis=1, concat_axis=0, tiled=True)  279 us
    all_to_all x1, waiting for transfers between devices, per_device(): lax.all_to_all(back_col, 'seq', split_axis=0, concat_axis=1, tiled=True)  269 us
    all_to_all x1, starting transfers between devices, per_device(): lax.all_to_all(mixed, 'seq', split_axis=1, concat_axis=0, tiled=True)  70.2 us
    all_to_all x1, starting transfers between devices, per_device(): lax.all_to_all(part_second.reshape(shards, shard_rows, extent), 'seq', sp...  70.2 us
    unnamed x15, local copies, waits for them, and re-layouts  49 us
    dot_general x1, matrix products, per_device(): jnp.einsum('ikc,kj->ijc', back_hidden, full_first, preferred_element_type...  36.2 us
    dot_general x1, matrix products, per_device(): jnp.einsum('ijc,kj->ikc', tokens_late, full_first, preferred_element_type...  28.2 us
    optimization_barrier x1, local copies, waits for them, and re-layouts, per_device(): mixed, back_rows = lax.optimization_barrier((mixed, back_rows))  26.5 us
  transfers between devices with their start and end apart: 8, of which 6 were waited for; matrix products, arithmetic and copies ran while one was open for 16% of the time, Pallas kernels for 0%

profile of v1, /device:TPU:0, one launch (start us, length us, event | category | flops | bytes accessed | tf_op | source)
XLA Modules:
  0.0 967.2 jit_solution(1456014706451392458)
XLA Ops:
  11.6 2.9 collective-permute-start.1
  14.6 3.8 collective-permute-done.1
  18.4 1.9 collective-permute-start.2
  20.3 6.1 collective-permute-done.2
  26.6 2.6 collective-permute-start.3
  29.1 18.4 %copy.21 = bf16[64,8,32,512]{3,1,2,0:T(8,128)(2,1)} copy(bf16[64,8,32,512]{3,2,1,0:T(8,128)(2,1)} %bitcast.58) | data formatting | bytes 33554432
  47.6 3.8 collective-permute-done.3
  51.8 18.2 %convolution_convert_fusion = bf16[512,16384]{1,0:T(8,128)(2,1)} fusion(bf16[512,16384]{1,0:T(8,128)(2,1)} %bitcast.53, bf16[2,512,512]{2,1,0:T(8,128)(2,1)S(1)} %maximum_select_fusion), kind=kOutput, calls=%fused_computation.9 | convolution fusion | flops 8598323200 | bytes 34078720 | tf_op jit(solution)/shard_map/dot_general | solution.py:47
  70.0 16.6 %copy.22 = bf16[64,8,32,512]{3,2,1,0:T(8,128)(2,1)} copy(bf16[64,8,32,512]{3,1,2,0:T(8,128)(2,1)} %bitcast.55) | data formatting | bytes 33554432
  86.5 5.6 all-to-all-start
  92.2 28.2 %fusion.4 = (bf16[32,512,512]{2,1,0:T(8,128)(2,1)}, f32[512,32,512]{2,0,1:T(8,128)}) fusion(bf16[32,512,512]{2,1,0:T(8,128)(2,1)} %param.7, f32[32,512]{1,0:T(8,128)S(1)} %convert_element_type.43, bf16[2,512,512]{2,1,0:T(8,128)(2,1)S(1)} %maximum_select_fusion), kind=kOutput, calls=%fused_computation.7 | convolution fusion | flops 8623489024 | bytes 84475904 | tf_op jit(solution)/shard_map/ijc,kj->ikc/dot_general | solution.py:55
  120.3 268.5 %all-to-all-done = bf16[512,32,512]{2,1,0:T(8,128)(2,1)} async-done(((bf16[512,32,512]{2,1,0:T(8,128)(2,1)}), bf16[512,32,512]{2,1,0:T(8,128)(2,1)}, u32[]{:S(2)}, u32[]{:S(2)}) %all-to-all-start) | async-done | bytes 16777248 | tf_op jit(solution)/shard_map/all_to_all | solution.py:51
  388.9 15.1 %copy.15 = bf16[16,32,32,512]{3,2,0,1:T(8,128)(2,1)} copy(bf16[16,32,32,512]{3,2,1,0:T(8,128)(2,1)} %bitcast.6) | data formatting | bytes 33554432 | tf_op jit(solution)/shard_map/all_to_all | solution.py:51
  404.0 1.8 copy-done
  405.8 26.5 %copy.17 = bf16[32,512,512]{2,0,1:T(8,128)(2,1)} copy(bf16[32,512,512]{2,1,0:T(8,128)(2,1)S(1)} %copy-done) | data formatting | bytes 33554432 | tf_op jit(solution)/shard_map/optimization_barrier | solution.py:57
  432.3 70.2 %all-to-all-start.1 = ((bf16[32,512,512]{2,0,1:T(8,128)(2,1)}), bf16[32,512,512]{2,0,1:T(8,128)(2,1)}, u32[]{:S(2)}, u32[]{:S(2)}) async-start(bf16[32,512,512]{2,0,1:T(8,128)(2,1)} %copy.17), calls=%async_computation.2 | async-start | bytes 33554432 | tf_op jit(solution)/shard_map/all_to_all | solution.py:58
  502.8 24.1 %fusion.11 = f32[512,512]{1,0:T(8,128)} fusion(bf16[32,512,512]{2,1,0:T(8,128)(2,1)} %param.7, bf16[32,512,512]{2,1,0:T(8,128)(2,1)} %bitcast.59, f32[32,512]{1,0:T(8,128)S(1)} %convert_element_type.43), kind=kOutput, calls=%fused_computation.12 | convolution fusion | flops 8631877632 | bytes 34668544 | tf_op jit(solution)/shard_map/ikc,ijc->kj/dot_general | solution.py:66
  526.9 278.7 %all-to-all-done.1 = bf16[32,512,512]{2,0,1:T(8,128)(2,1)} async-done(((bf16[32,512,512]{2,0,1:T(8,128)(2,1)}), bf16[32,512,512]{2,0,1:T(8,128)(2,1)}, u32[]{:S(2)}, u32[]{:S(2)}) %all-to-all-start.1) | async-done | bytes 16777248 | tf_op jit(solution)/shard_map/all_to_all | solution.py:58
  805.7 15.8 %copy.18 = bf16[32,16,32,512]{3,2,0,1:T(8,128)(2,1)S(1)} copy(bf16[32,16,32,512]{3,0,2,1:T(8,128)(2,1)} %bitcast.12) | data formatting | bytes 33554432 | tf_op jit(solution)/shard_map/all_to_all | solution.py:58
  821.5 12.2 %copy.23 = bf16[64,8,32,512]{3,1,2,0:T(8,128)(2,1)} copy(bf16[64,8,32,512]{3,2,1,0:T(8,128)(2,1)S(1)} %bitcast.57) | data formatting | bytes 33554432
  833.7 18.0 %fusion.36 = f32[512,512]{0,1:T(8,128)} fusion(bf16[512,16384]{1,0:T(8,128)(2,1)} %bitcast.61, bf16[512,16384]{1,0:T(8,128)(2,1)} %bitcast.54), kind=kOutput, calls=%fused_computation.50 | convolution fusion | flops 8589934592 | bytes 34603008 | tf_op jit(solution)/shard_map/dot_general | solution.py:71
  851.7 70.2 %all-to-all-start.2 = ((f32[16,32,512]{2,1,0:T(8,128)}), f32[16,32,512]{2,1,0:T(8,128)S(1)}, u32[]{:S(2)}, u32[]{:S(2)}) async-start(f32[16,32,512]{2,1,0:T(8,128)} %bitcast.15), calls=%async_computation.3 | async-start | bytes 2097152 | tf_op jit(solution)/shard_map/all_to_all | solution.py:74
  922.0 36.2 %fusion.2 = bf16[32,512,512]{2,1,0:T(8,128)(2,1)} fusion(bf16[32,512,512]{2,1,0:T(8,128)(2,1)} %bitcast.60, f32[512,32,512]{2,0,1:T(8,128)} %get-tuple-element.10, f32[32,512]{1,0:T(8,128)S(1)} %convert_element_type.43, bf16[32,512,512]{2,1,0:T(8,128)(2,1)} %param.7, bf16[2,512,512]{2,1,0:T(8,128)(2,1)S(1)} %maximum_select_fusion), kind=kOutput, calls=%fused_computation.4 | convolution fusion | flops 8673820672 | bytes 101318656 | tf_op jit(solution)/shard_map/ikc,kj->ijc/dot_general | solution.py:63
  958.2 1.5 multiply_multiply_fusion.1
  (30 shorter events, 6.2 us)
Async XLA Ops:
  8.3 6.3 copy-start.1
  9.3 5.2 copy-start.3
  10.2 1.4 collective-permute-start
  11.6 6.8 collective-permute-start.1
  18.4 7.9 collective-permute-start.2
  26.6 24.8 %collective-permute-start.3 = (bf16[2,256,512]{2,1,0:T(8,128)(2,1)S(1)}, bf16[2,256,512]{2,1,0:T(8,128)(2,1)S(1)}, u32[]{:S(2)}, u32[]{:S(2)}) collective-permute-start(bf16[2,256,512]{2,1,0:T(8,128)(2,1)S(1)} %maximum_select_fusion.1), channel_id=1, source_target_pairs={{0,8},{1,9},{2,10},{3,11},{4,12},{5,13},{6,14},{7,15},{8,0},{9,1},... | collective-permute-start | bytes 1572872 | tf_op jit(solution)/shard_map/ppermute | solution.py:14
  86.5 5.6 copy-start.5
  86.5 302.3 %all-to-all-start = ((bf16[512,32,512]{2,1,0:T(8,128)(2,1)}), bf16[512,32,512]{2,1,0:T(8,128)(2,1)}, u32[]{:S(2)}, u32[]{:S(2)}) async-start(bf16[512,32,512]{2,1,0:T(8,128)(2,1)} %bitcast.56), calls=%async_computation | async-start | bytes 33554432 | tf_op jit(solution)/shard_map/all_to_all | solution.py:51
  388.9 16.9 %copy-start = (bf16[32,512,512]{2,1,0:T(8,128)(2,1)S(1)}, bf16[32,512,512]{2,1,0:T(8,128)(2,1)}, u32[]{:S(2)}) copy-start(bf16[32,512,512]{2,1,0:T(8,128)(2,1)} %get-tuple-element.8) | copy-start | bytes 50331652
  432.3 373.4 %all-to-all-start.1 = ((bf16[32,512,512]{2,0,1:T(8,128)(2,1)}), bf16[32,512,512]{2,0,1:T(8,128)(2,1)}, u32[]{:S(2)}, u32[]{:S(2)}) async-start(bf16[32,512,512]{2,0,1:T(8,128)(2,1)} %copy.17), calls=%async_computation.2 | async-start | bytes 33554432 | tf_op jit(solution)/shard_map/all_to_all | solution.py:58
  502.5 455.6 %reduce-scatter.2.cloned.1.call-start = ((), (), s32[]{:S(2)}) async-start(), calls=%async_computation.4 | async-start | bytes 1114112 | tf_op jit(solution)/shard_map/reduce_scatter | solution.py:65
  851.7 107.9 %all-to-all-start.2 = ((f32[16,32,512]{2,1,0:T(8,128)}), f32[16,32,512]{2,1,0:T(8,128)S(1)}, u32[]{:S(2)}, u32[]{:S(2)}) async-start(f32[16,32,512]{2,1,0:T(8,128)} %bitcast.15), calls=%async_computation.3 | async-start | bytes 2097152 | tf_op jit(solution)/shard_map/all_to_all | solution.py:74
  922.0 36.2 %copy-start.4 = (f32[32,512]{1,0:T(8,128)S(1)}, f32[32,512]{1,0:T(8,128)}, u32[]{:S(2)}) copy-start(f32[32,512]{1,0:T(8,128)} %copy-done.3) | copy-start | bytes 196612
  922.0 37.7 %copy-start.2 = (f32[32,512]{1,0:T(8,128)S(1)}, f32[32,512]{1,0:T(8,128)}, u32[]{:S(2)}) copy-start(f32[32,512]{1,0:T(8,128)} %copy-done.1) | copy-start | bytes 196612
Sparse Core Ops, SparseCore 0:
  527.1 257.9 reduce-scatter.1
